TPU v7x, 32 devices: a whole 2x2x4 slice. The times are simulated.
32 devices in a mesh: expert: 16 (over z, x, core), tensor: 2 (over y).
Axes of the slice: x: 2, y: 2, z: 4, core: 2. Of those that a mesh axis runs over, the one named last changes fastest.
Arguments:
- query: bfloat16 [128, 8192], P(('expert', 'tensor')), may hold values from -6 to 6
- cache_keys: bfloat16 [128, 128, 4, 128], P(('expert', 'tensor')), may hold values from -6 to 6
- cache_values: bfloat16 [128, 128, 4, 128], P(('expert', 'tensor')), may hold values from -6 to 6
- lengths: int32 [128], P(('expert', 'tensor')), may hold values from 2 to 128, as said below
- residual: bfloat16 [128, 4096], P('tensor', 'expert'), may hold values from -12 to 12
- out_proj: bfloat16 [4096, 8192], P('expert', 'tensor'), may hold values from -0.0625 to 0.0625
- norm_gain: bfloat16 [4096], P('expert'), may hold values from 0.099609375 to 1.8984375
- expert_ids: int32 [128, 8], replicated, may hold values from 0 to 15, all different within a row; in each aligned block of 128 rows (0 to 127, 128 to 255, ...) at most 128 rows name the same one
- gate_scores: bfloat16 [128, 8], replicated, may hold values from 0.019897461 to 1
- w_gate: bfloat16 [16, 1536, 4096], P('expert', 'tensor'), may hold values from -0.09375 to 0.09375
- w_up: bfloat16 [16, 1536, 4096], P('expert', 'tensor'), may hold values from -0.09375 to 0.09375
- w_down: bfloat16 [16, 1536, 4096], P('expert', 'tensor'), may hold values from -0.15625 to 0.15625
Outputs:
- attn_residual: bfloat16 [128, 4096], P('tensor', 'expert')
- expert_mix: bfloat16 [128, 4096], P('tensor', 'expert')
Inputs may be any that keep to these rules, and one draw needn't show every extreme that they name: `expert_ids`: each row names 8 different experts; no expert is named by more than 128 rows, and one by exactly 128. `lengths`: some row has exactly 128.
All inputs are finite; a program needn't handle non-finite values.
Results may differ from a plain program's by a relative error of at most 0.018.
Values may be sent and summed in bfloat16 or wider, within the bound.
A program may use at most 64 MiB of HBM per device.

v0:
```python
import jax
import jax.numpy as jnp
from jax import lax
from jax.sharding import PartitionSpec as P

floor_value = -1e30
epsilon = 1e-06


def softmax_parts(queries, key_block, value_block, usable, score_scale):
    scores = (
        jnp.einsum("rkgd,rpkd->rkgp", queries, key_block, preferred_element_type=jnp.float32)
        * score_scale
    )
    usable_mask = usable[:, None, None, :]
    peak = jnp.max(jnp.where(usable_mask, scores, floor_value), axis=-1)
    raw_weights = jnp.where(usable_mask, jnp.exp(scores - peak[..., None]), 0.0)
    weight_sum = jnp.sum(raw_weights, axis=-1)
    weighted = jnp.einsum("rkgp,rpkd->rkgd", raw_weights, value_block.astype(jnp.float32))
    return (weight_sum, weighted)


def body(
    query,
    cache_keys,
    cache_values,
    lengths,
    residual,
    out_proj,
    norm_gain,
    expert_ids,
    gate_scores,
    w_gate,
    w_up,
    w_down,
):
    row_count, full_heads_width = query.shape
    cache_len = cache_keys.shape[1]
    kv_count = cache_keys.shape[2]
    head_size = cache_keys.shape[3]
    head_count = full_heads_width // head_size
    group_size = head_count // kv_count
    score_scale = head_size ** (-0.5)
    usable = jnp.arange(cache_len, dtype=jnp.int32)[None, :] < lengths[:, None]
    grouped = query.reshape(row_count, kv_count, group_size, head_size)
    weight_sum, weighted = softmax_parts(grouped, cache_keys, cache_values, usable, score_scale)
    context_rows_own = (
        (weighted / weight_sum[..., None]).astype(jnp.bfloat16).reshape(row_count, full_heads_width)
    )
    context = lax.all_to_all(context_rows_own, "tensor", split_axis=1, concat_axis=0, tiled=True)
    attn_part = jnp.dot(
        lax.all_gather(context, "expert", axis=0, tiled=True),
        out_proj.T,
        preferred_element_type=jnp.float32,
    )
    attn_share = lax.psum_scatter(attn_part, "tensor", scatter_dimension=0, tiled=True)
    hidden_state = residual.astype(jnp.float32) + attn_share
    squares = lax.psum(jnp.sum(hidden_state * hidden_state, axis=1), "expert")
    full_width = hidden_state.shape[1] * lax.axis_size("expert")
    scaled_share = (hidden_state * norm_gain.astype(jnp.float32)[None, :]).astype(jnp.bfloat16)
    scaled = lax.all_gather(
        lax.all_gather(scaled_share, "tensor", axis=0, tiled=True), "expert", axis=1, tiled=True
    )
    mean_all = lax.all_gather(squares / full_width, "tensor", axis=0, tiled=True)
    row_scale = lax.rsqrt(mean_all + epsilon)[:, None]
    experts_local = w_gate.shape[0]
    gate_weight = gate_scores.astype(jnp.float32)
    gate_weight = gate_weight / jnp.sum(gate_weight, axis=1, keepdims=True)
    mixed = None
    for local in range(experts_local):
        expert = lax.axis_index("expert") * experts_local + local
        weight = jnp.sum(jnp.where(expert_ids == expert, gate_weight, 0.0), axis=1, keepdims=True)
        gate_proj = row_scale * lax.dot_general(
            scaled, w_gate[local], (((1,), (1,)), ((), ())), preferred_element_type=jnp.float32
        )
        up_proj = row_scale * lax.dot_general(
            scaled, w_up[local], (((1,), (1,)), ((), ())), preferred_element_type=jnp.float32
        )
        activation = (jax.nn.silu(gate_proj) * up_proj).astype(jnp.bfloat16)
        part = weight * jnp.dot(activation, w_down[local], preferred_element_type=jnp.float32)
        mixed = part if mixed is None else mixed + part
    mixed = lax.psum_scatter(mixed.astype(jnp.bfloat16), "tensor", scatter_dimension=0, tiled=True)
    mixed_share = lax.psum_scatter(mixed, "expert", scatter_dimension=1, tiled=True)
    return (hidden_state.astype(jnp.bfloat16), mixed_share)


def solution(mesh):
    in_specs = (
        P(("expert", "tensor"), None),
        P(("expert", "tensor"), None, None, None),
        P(("expert", "tensor"), None, None, None),
        P(("expert", "tensor")),
        P("tensor", "expert"),
        P("expert", "tensor"),
        P("expert"),
        P(),
        P(),
        P("expert", "tensor", None),
        P("expert", "tensor", None),
        P("expert", "tensor", None),
    )
    out_specs = (P("tensor", "expert"), P("tensor", "expert"))
    return jax.shard_map(body, mesh=mesh, in_specs=in_specs, out_specs=out_specs, check_vma=False)
```

profile of v0, /device:TPU:0, one launch (start us, length us, event | category | flops | bytes accessed | tf_op | source)
XLA Modules:
  0.0 218.9 jit_solution(551768819832569103)
XLA Ops:
  7.2 0.0 copy-start
  7.2 0.0 all-gather.3.cloned.1.call-start
  7.3 0.9 iota_compare_fusion
  8.1 0.8 copy.19
  9.0 1.5 select_reduce_fusion
  10.5 2.5 %fusion = f32[4,4,16,128]{3,2,1,0:T(8,128)S(1)} fusion(f32[4,4,16,128]{3,2,1,0:T(8,128)S(1)} %get-tuple-element.6, f32[4,4,16]{2,1,0:T(4,128)S(1)} %get-tuple-element.5, pred[4,128]{1,0:T(4,128)(4,1)S(1)} %iota_compare_fusion), kind=kOutput, calls=%fused_computation | output fusion | flops 65919 | bytes 263680 | tf_op jit(solution)/shard_map/div | solution.py:48
  13.0 1.4 fusion.25
  14.4 0.1 copy.18
  14.5 8.2 %all_to_all.19 = bf16[4,2,4096]{2,0,1:T(4,128)(2,1)S(1)} all-to-all(bf16[4,2,4096]{2,0,1:T(4,128)(2,1)S(1)} %copy.18), channel_id=1, replica_groups=mesh['expert'=16,'tensor'=2] {'tensor'}, dimensions={1} | all-to-all | bytes 131072 | tf_op jit(solution)/shard_map/all_to_all | solution.py:50
  22.7 0.6 all_to_all.17
  23.3 0.0 all-gather.3.cloned.1.call-update
  23.3 0.0 reduce-scatter.4.cloned.1.call-start
  23.4 38.2 %all-gather.3.cloned.1.call-done = bf16[128,4096]{1,0:T(8,128)(2,1)} async-done(((bf16[8,4096]{1,0:T(8,128)(2,1)}), bf16[128,4096]{1,0:T(8,128)(2,1)}) %all-gather.3.cloned.1.call-update) | async-done | bytes 1048592 | tf_op jit(solution)/shard_map/all_gather | solution.py:52
  61.6 2.7 %fusion.50 = f32[128,256]{1,0:T(8,128)} fusion(bf16[128,4096]{1,0:T(8,128)(2,1)} %all-gather.3.cloned.1.call-done, bf16[256,4096]{1,0:T(8,128)(2,1)S(1)} %copy-done), kind=kOutput, calls=%fused_computation.48 | convolution fusion | flops 268435456 | bytes 3276800 | tf_op jit(solution)/shard_map/dot_general | solution.py:51
  64.3 0.0 reduce-scatter.4.cloned.1.call-update
  64.3 0.0 all-gather.5.cloned.1.call-start
  64.4 9.4 %reduce-scatter.4.cloned.1.call-done = f32[64,256]{1,0:T(8,128)} async-done(((f32[128,256]{1,0:T(8,128)}), f32[64,256]{1,0:T(8,128)}) %reduce-scatter.4.cloned.1.call-update) | async-done | bytes 65552 | tf_op jit(solution)/shard_map/reduce_scatter | solution.py:56
  73.8 1.6 multiply_reduce_fusion
  75.4 4.7 %all_gather.14 = bf16[128,256]{1,0:T(8,128)(2,1)} all-gather(bf16[64,256]{1,0:T(8,128)(2,1)S(1)} %get-tuple-element.3), channel_id=1, replica_groups=mesh['expert'=16,'tensor'=2] {'tensor'}, dimensions={0}, use_global_device_ids=true | all-gather | bytes 98304 | tf_op jit(solution)/shard_map/all_gather | solution.py:62
  80.1 0.0 all-gather.5.cloned.1.call-update
  80.1 0.0 reduce-scatter.6.cloned.1.call-start
  80.2 0.6 dynamic-slice
  81.5 31.9 %psum.7 = f32[64]{0:T(128)S(1)} all-reduce(f32[64]{0:T(128)S(1)} %get-tuple-element.2), channel_id=1, replica_groups=mesh['expert'=16,'tensor'=2] {'expert'}, use_global_device_ids=true, to_apply=%region_6.7 | all-reduce | flops 64 | bytes 512 | tf_op jit(solution)/shard_map/psum | solution.py:58
  113.4 0.1 multiply_dynamic-update-slice_fusion
  113.5 4.9 %all-reduce = f32[128]{0:T(128)S(1)} all-reduce(f32[128]{0:T(128)S(1)} %multiply_dynamic-update-slice_fusion), channel_id=1, replica_groups=mesh['expert'=16,'tensor'=2] {'tensor'}, use_global_device_ids=true, to_apply=%add | all-reduce | flops 128 | bytes 1024
  118.5 5.4 %fusion.13 = f32[128,768]{1,0:T(8,128)S(1)} fusion(bf16[128,4096]{1,0:T(8,128)(2,1)} %all-gather.5.cloned.1.call-done, bf16[1,768,4096]{2,1,0:T(8,128)(2,1)} %param.21, f32[128]{0:T(128)S(1)} %add_rsqrt_fusion), kind=kOutput, calls=%fused_computation.9 | convolution fusion | flops 805404672 | bytes 7733760 | tf_op jit(solution)/shard_map/dot_general | solution.py:73
  123.9 9.7 %fusion.10 = bf16[128,4096]{1,0:T(8,128)(2,1)} fusion(bf16[1,768,4096]{2,1,0:T(8,128)(2,1)} %param.23, f32[128]{0:T(128)S(1)} %fusion.46, bf16[128,4096]{1,0:T(8,128)(2,1)S(1)} %copy-done.1, bf16[1,768,4096]{2,1,0:T(8,128)(2,1)} %param.22, f32[128,768]{1,0:T(8,128)S(1)} %fusion.13, f32[128]{0:T(128)S(1)} %add_rsqrt_fusion), kind=kOutput, calls=%fused_computation.8 | convolution fusion | flops 1612349440 | bytes 15074304 | tf_op jit(solution)/shard_map/dot_general | solution.py:80
  133.5 0.0 reduce-scatter.6.cloned.1.call-update
  133.6 0.0 reduce-scatter.8.cloned.1.call-start
  133.6 18.6 %reduce-scatter.6.cloned.1.call-done = bf16[64,4096]{1,0:T(8,128)(2,1)} async-done(((bf16[128,4096]{1,0:T(8,128)(2,1)}), bf16[64,4096]{1,0:T(8,128)(2,1)}) %reduce-scatter.6.cloned.1.call-update) | async-done | bytes 524304 | tf_op jit(solution)/shard_map/reduce_scatter | solution.py:82
  152.2 0.0 reduce-scatter.8.cloned.1.call-update
  152.2 60.1 %reduce-scatter.8.cloned.1.call-done = bf16[64,256]{1,0:T(8,128)(2,1)} async-done(((bf16[64,4096]{1,0:T(8,128)(2,1)}), bf16[64,256]{1,0:T(8,128)(2,1)}) %reduce-scatter.8.cloned.1.call-update) | async-done | bytes 32784 | tf_op jit(solution)/shard_map/reduce_scatter | solution.py:83
  (20 shorter events, 0.1 us)
Async XLA Ops:
  7.2 54.4 %copy-start = (bf16[256,4096]{1,0:T(8,128)(2,1)S(1)}, bf16[256,4096]{1,0:T(8,128)(2,1)}, u32[]{:S(2)}) copy-start(bf16[256,4096]{1,0:T(8,128)(2,1)} %param.17) | copy-start | bytes 6291460
  7.2 73.0 %copy-start.6 = (u32[32]{0:T(128)S(1)}, u32[32]{0:T(128)}, u32[]{:S(2)}) copy-start(u32[32]{0:T(128)} %constant.31) | copy-start | bytes 388
  7.2 57.2 %copy-start.5 = (bf16[256]{0:T(256)(128)(2,1)S(1)}, bf16[256]{0:T(256)(128)(2,1)}, u32[]{:S(2)}) copy-start(bf16[256]{0:T(256)(128)(2,1)} %param.18) | copy-start | bytes 1540
  7.2 66.6 %copy-start.2 = (bf16[64,256]{1,0:T(8,128)(2,1)S(1)}, bf16[64,256]{1,0:T(8,128)(2,1)}, u32[]{:S(2)}) copy-start(bf16[64,256]{1,0:T(8,128)(2,1)} %param.16) | copy-start | bytes 98308
  7.2 74.2 %copy-start.3 = (bf16[128,8]{0,1:T(8,128)(2,1)S(1)}, bf16[128,8]{0,1:T(8,128)(2,1)}, u32[]{:S(2)}) copy-start(bf16[128,8]{0,1:T(8,128)(2,1)} %param.20) | copy-start | bytes 6148
  7.2 74.2 %copy-start.4 = (s32[128,8]{0,1:T(8,128)S(1)}, s32[128,8]{0,1:T(8,128)}, u32[]{:S(2)}) copy-start(s32[128,8]{0,1:T(8,128)} %param.19) | copy-start | bytes 12292
  7.2 54.4 %all-gather.3.cloned.1.call-start = ((), (), s32[]{:S(2)}) async-start(), calls=%async_computation.4 | async-start | bytes 1114112 | tf_op jit(solution)/shard_map/all_gather | solution.py:52
  23.3 50.5 %reduce-scatter.4.cloned.1.call-start = ((), (), s32[]{:S(2)}) async-start(), calls=%async_computation.5 | async-start | bytes 196608 | tf_op jit(solution)/shard_map/reduce_scatter | solution.py:56
  64.3 54.1 %all-gather.5.cloned.1.call-start = ((), (), s32[]{:S(2)}) async-start(), calls=%async_computation.6 | async-start | bytes 1114112 | tf_op jit(solution)/shard_map/all_gather | solution.py:61
  80.1 72.1 %reduce-scatter.6.cloned.1.call-start = ((), (), s32[]{:S(2)}) async-start(), calls=%async_computation.7 | async-start | bytes 1572864 | tf_op jit(solution)/shard_map/reduce_scatter | solution.py:82
  118.5 5.4 %copy-start.1 = (bf16[128,4096]{1,0:T(8,128)(2,1)S(1)}, bf16[128,4096]{1,0:T(8,128)(2,1)}, u32[]{:S(2)}) copy-start(bf16[128,4096]{1,0:T(8,128)(2,1)} %all-gather.5.cloned.1.call-done) | copy-start | bytes 3145732
  133.6 78.8 %reduce-scatter.8.cloned.1.call-start = ((), (), s32[]{:S(2)}) async-start(), calls=%async_computation.8 | async-start | bytes 557056 | tf_op jit(solution)/shard_map/reduce_scatter | solution.py:83
Sparse Core Ops, SparseCore 0:
  23.4 38.1 all-gather.2
  64.5 9.3 reduce-scatter.3
  80.3 36.6 all-gather.4
  133.7 18.4 reduce-scatter.5
  156.2 56.1 reduce-scatter.7
where the time goes:
time: 219 us
  waiting for transfers between devices  126 us (58%)
  blocking collectives  49.7 us (23%)
  matrix products  20.7 us (9%)
  between operations  14.6 us (7%)
  other arithmetic  5.06 us (2%)
  local copies, waits for them, and re-layouts  2.19 us (1%)
    reduce_scatter x1, waiting for transfers between devices, body(): lax.psum_scatter(mixed, 'expert', scatter_dimension=1, tiled=True)  60.1 us
    all_gather x1, waiting for transfers between devices, body(): lax.all_gather(context, 'expert', axis=0, tiled=True)  38.2 us
    psum x1, blocking collectives, body(): squares = lax.psum(jnp.sum(hidden_state * hidden_state, axis=1), 'expert')  31.9 us
    reduce_scatter x1, waiting for transfers between devices, body(): lax.psum_scatter(mixed.astype(jnp.bfloat16), 'tensor', scatter_dimension=...  18.6 us
    dot_general x1, matrix products, body(): jnp.dot(activation, w_down[local], preferred_element_type=jnp.float32)  9.66 us
    reduce_scatter x1, waiting for transfers between devices, body(): lax.psum_scatter(attn_part, 'tensor', scatter_dimension=0, tiled=True)  9.44 us
    all_to_all x1, blocking collectives, body(): lax.all_to_all(context_rows_own, 'tensor', split_axis=1, concat_axis=0, t...  8.18 us
    dot_general x1, matrix products, body(): lax.dot_general(scaled, w_gate[local], (((1,), (1,)), ((), ())), preferre...  5.4 us
  transfers between devices with their start and end apart: 5, of which 4 were waited for; matrix products, arithmetic and copies ran while one was open for 0% of the time, Pallas kernels for 0%

commit v1 on v0

--- a/solution.py
+++ b/solution.py
@@ -49,7 +49,9 @@
     )
     context = lax.all_to_all(context_rows_own, "tensor", split_axis=1, concat_axis=0, tiled=True)
     attn_part = jnp.dot(
-        lax.all_gather(context, "expert", axis=0, tiled=True),
+        jnp.concatenate(
+            lax.all_to_all(jnp.stack([context] * lax.axis_size("expert")), "expert", 0, 0), axis=0
+        ),
         out_proj.T,
         preferred_element_type=jnp.float32,
     )

time: 219 us -> 210 us (0.959)
  waiting for transfers between devices: 126 us -> 88.7 us
  blocking collectives: 49.7 us -> 80.1 us
    all_gather x1 -> x0, waiting for transfers between devices: 38.2 us -> none  [body(): lax.all_gather(context, 'expert', axis=0, tiled=True)]
    all_to_all x0 -> x1, blocking collectives: none -> 30.4 us  [body(): lax.all_to_all(jnp.stack([context] * lax.axis_size('expert')), 'expert',...]
  transfers between devices with their start and end apart: 5 -> 4, of which waited for: 4 -> 3; matrix products, arithmetic and copies ran while one was open for 0% -> 0% of each run, Pallas kernels for 0% -> 0%
where the time goes in v1:
time: 210 us
  waiting for transfers between devices  88.7 us (42%)
  blocking collectives  80.1 us (38%)
  matrix products  19.4 us (9%)
  between operations  14.6 us (7%)
  other arithmetic  5.06 us (2%)
    reduce_scatter x1, waiting for transfers between devices, body(): lax.psum_scatter(mixed, 'expert', scatter_dimension=1, tiled=True)  60.2 us
    psum x1, blocking collectives, body(): squares = lax.psum(jnp.sum(hidden_state * hidden_state, axis=1), 'expert')  31.9 us
    all_to_all x1, blocking collectives, body(): lax.all_to_all(jnp.stack([context] * lax.axis_size('expert')), 'expert',...  30.4 us
    reduce_scatter x1, waiting for transfers between devices, body(): lax.psum_scatter(mixed.astype(jnp.bfloat16), 'tensor', scatter_dimension=...  18.6 us
    reduce_scatter x1, waiting for transfers between devices, body(): lax.psum_scatter(attn_part, 'tensor', scatter_dimension=0, tiled=True)  9.92 us
    dot_general x1, matrix products, body(): jnp.dot(activation, w_down[local], preferred_element_type=jnp.float32)  9.67 us
    all_to_all x1, blocking collectives, body(): lax.all_to_all(context_rows_own, 'tensor', split_axis=1, concat_axis=0, t...  8.18 us
    dot_general x1, matrix products, body(): lax.dot_general(scaled, w_gate[local], (((1,), (1,)), ((), ())), preferre...  5.4 us
  transfers between devices with their start and end apart: 4, of which 3 were waited for; matrix products, arithmetic and copies ran while one was open for 0% of the time, Pallas kernels for 0%

profile of v1, /device:TPU:0, one launch (start us, length us, event | category | flops | bytes accessed | tf_op | source)
XLA Modules:
  0.0 209.7 jit_solution(3295761533697509364)
XLA Ops:
  7.2 0.0 copy-start
  7.2 0.0 copy-start.6
  7.2 0.0 copy-start.5
  7.2 0.0 reduce-scatter.4.cloned.1.call-start
  7.3 0.9 iota_compare_fusion
  8.1 0.8 copy.19
  9.0 1.5 select_reduce_fusion
  10.5 2.5 %fusion = f32[4,4,16,128]{3,2,1,0:T(8,128)S(1)} fusion(f32[4,4,16,128]{3,2,1,0:T(8,128)S(1)} %get-tuple-element.6, f32[4,4,16]{2,1,0:T(4,128)S(1)} %get-tuple-element.5, pred[4,128]{1,0:T(4,128)(4,1)S(1)} %iota_compare_fusion), kind=kOutput, calls=%fused_computation | output fusion | flops 65919 | bytes 263680 | tf_op jit(solution)/shard_map/div | solution.py:48
  13.0 1.4 fusion.25
  14.4 0.1 copy.18
  14.5 8.2 %all_to_all.21 = bf16[4,2,4096]{2,0,1:T(4,128)(2,1)S(1)} all-to-all(bf16[4,2,4096]{2,0,1:T(4,128)(2,1)S(1)} %copy.18), channel_id=1, replica_groups=mesh['expert'=16,'tensor'=2] {'tensor'}, dimensions={1} | all-to-all | bytes 131072 | tf_op jit(solution)/shard_map/all_to_all | solution.py:50
  22.7 0.1 stack.5
  22.8 30.4 %all_to_all.22 = bf16[16,8,4096]{2,1,0:T(8,128)(2,1)S(1)} all-to-all(bf16[16,8,4096]{2,1,0:T(8,128)(2,1)S(1)} %stack.5), channel_id=1, replica_groups=mesh['expert'=16,'tensor'=2] {'expert'}, dimensions={0} | all-to-all | bytes 2097152 | tf_op jit(solution)/shard_map/all_to_all | solution.py:53
  53.2 1.5 fusion.26
  54.7 0.0 reduce-scatter.4.cloned.1.call-update
  54.7 0.0 all-gather.2.cloned.1.call-start
  54.7 9.9 %reduce-scatter.4.cloned.1.call-done = f32[64,256]{1,0:T(8,128)} async-done(((f32[128,256]{1,0:T(8,128)}), f32[64,256]{1,0:T(8,128)}) %reduce-scatter.4.cloned.1.call-update) | async-done | bytes 65552 | tf_op jit(solution)/shard_map/reduce_scatter | solution.py:58
  64.7 1.6 multiply_reduce_fusion
  66.2 4.7 %all_gather.10 = bf16[128,256]{1,0:T(8,128)(2,1)} all-gather(bf16[64,256]{1,0:T(8,128)(2,1)S(1)} %get-tuple-element.3), channel_id=1, replica_groups=mesh['expert'=16,'tensor'=2] {'tensor'}, dimensions={0}, use_global_device_ids=true | all-gather | bytes 98304 | tf_op jit(solution)/shard_map/all_gather | solution.py:64
  70.9 0.0 all-gather.2.cloned.1.call-update
  71.0 0.0 reduce-scatter.6.cloned.1.call-start
  71.0 0.6 dynamic-slice
  72.3 31.9 %psum.7 = f32[64]{0:T(128)S(1)} all-reduce(f32[64]{0:T(128)S(1)} %get-tuple-element.2), channel_id=1, replica_groups=mesh['expert'=16,'tensor'=2] {'expert'}, use_global_device_ids=true, to_apply=%region_6.7 | all-reduce | flops 64 | bytes 512 | tf_op jit(solution)/shard_map/psum | solution.py:60
  104.3 0.1 multiply_dynamic-update-slice_fusion
  104.3 4.9 %all-reduce = f32[128]{0:T(128)S(1)} all-reduce(f32[128]{0:T(128)S(1)} %multiply_dynamic-update-slice_fusion), channel_id=1, replica_groups=mesh['expert'=16,'tensor'=2] {'tensor'}, use_global_device_ids=true, to_apply=%add | all-reduce | flops 128 | bytes 1024
  109.3 5.4 %fusion.13 = f32[128,768]{1,0:T(8,128)S(1)} fusion(bf16[128,4096]{1,0:T(8,128)(2,1)} %all-gather.2.cloned.1.call-done, bf16[1,768,4096]{2,1,0:T(8,128)(2,1)} %param.21, f32[128]{0:T(128)S(1)} %add_rsqrt_fusion), kind=kOutput, calls=%fused_computation.9 | convolution fusion | flops 805404672 | bytes 7733760 | tf_op jit(solution)/shard_map/dot_general | solution.py:75
  114.7 9.7 %fusion.10 = bf16[128,4096]{1,0:T(8,128)(2,1)} fusion(bf16[1,768,4096]{2,1,0:T(8,128)(2,1)} %param.23, f32[128]{0:T(128)S(1)} %fusion.48, bf16[128,4096]{1,0:T(8,128)(2,1)S(1)} %copy-done.1, bf16[1,768,4096]{2,1,0:T(8,128)(2,1)} %param.22, f32[128,768]{1,0:T(8,128)S(1)} %fusion.13, f32[128]{0:T(128)S(1)} %add_rsqrt_fusion), kind=kOutput, calls=%fused_computation.8 | convolution fusion | flops 1612349440 | bytes 15074304 | tf_op jit(solution)/shard_map/dot_general | solution.py:82
  124.4 0.0 reduce-scatter.6.cloned.1.call-update
  124.4 0.0 reduce-scatter.8.cloned.1.call-start
  124.4 18.6 %reduce-scatter.6.cloned.1.call-done = bf16[64,4096]{1,0:T(8,128)(2,1)} async-done(((bf16[128,4096]{1,0:T(8,128)(2,1)}), bf16[64,4096]{1,0:T(8,128)(2,1)}) %reduce-scatter.6.cloned.1.call-update) | async-done | bytes 524304 | tf_op jit(solution)/shard_map/reduce_scatter | solution.py:84
  143.0 0.0 reduce-scatter.8.cloned.1.call-update
  143.0 60.2 %reduce-scatter.8.cloned.1.call-done = bf16[64,256]{1,0:T(8,128)(2,1)} async-done(((bf16[64,4096]{1,0:T(8,128)(2,1)}), bf16[64,256]{1,0:T(8,128)(2,1)}) %reduce-scatter.8.cloned.1.call-update) | async-done | bytes 32784 | tf_op jit(solution)/shard_map/reduce_scatter | solution.py:85
  (19 shorter events, 0.1 us)
Async XLA Ops:
  7.2 46.0 %copy-start = (bf16[256,4096]{1,0:T(8,128)(2,1)S(1)}, bf16[256,4096]{1,0:T(8,128)(2,1)}, u32[]{:S(2)}) copy-start(bf16[256,4096]{1,0:T(8,128)(2,1)} %param.17) | copy-start | bytes 6291460
  7.2 63.8 %copy-start.6 = (u32[32]{0:T(128)S(1)}, u32[32]{0:T(128)}, u32[]{:S(2)}) copy-start(u32[32]{0:T(128)} %constant.31) | copy-start | bytes 388
  7.2 47.5 %copy-start.5 = (bf16[256]{0:T(256)(128)(2,1)S(1)}, bf16[256]{0:T(256)(128)(2,1)}, u32[]{:S(2)}) copy-start(bf16[256]{0:T(256)(128)(2,1)} %param.18) | copy-start | bytes 1540
  7.2 57.5 %copy-start.2 = (bf16[64,256]{1,0:T(8,128)(2,1)S(1)}, bf16[64,256]{1,0:T(8,128)(2,1)}, u32[]{:S(2)}) copy-start(bf16[64,256]{1,0:T(8,128)(2,1)} %param.16) | copy-start | bytes 98308
  7.2 65.0 %copy-start.3 = (bf16[128,8]{0,1:T(8,128)(2,1)S(1)}, bf16[128,8]{0,1:T(8,128)(2,1)}, u32[]{:S(2)}) copy-start(bf16[128,8]{0,1:T(8,128)(2,1)} %param.20) | copy-start | bytes 6148
  7.2 65.1 %copy-start.4 = (s32[128,8]{0,1:T(8,128)S(1)}, s32[128,8]{0,1:T(8,128)}, u32[]{:S(2)}) copy-start(s32[128,8]{0,1:T(8,128)} %param.19) | copy-start | bytes 12292
  7.2 57.4 %reduce-scatter.4.cloned.1.call-start = ((), (), s32[]{:S(2)}) async-start(), calls=%async_computation.5 | async-start | bytes 196608 | tf_op jit(solution)/shard_map/reduce_scatter | solution.py:58
  54.7 54.6 %all-gather.2.cloned.1.call-start = ((), (), s32[]{:S(2)}) async-start(), calls=%async_computation.6 | async-start | bytes 1114112 | tf_op jit(solution)/shard_map/all_gather | solution.py:63
  71.0 72.1 %reduce-scatter.6.cloned.1.call-start = ((), (), s32[]{:S(2)}) async-start(), calls=%async_computation.7 | async-start | bytes 1572864 | tf_op jit(solution)/shard_map/reduce_scatter | solution.py:84
  109.3 5.4 %copy-start.1 = (bf16[128,4096]{1,0:T(8,128)(2,1)S(1)}, bf16[128,4096]{1,0:T(8,128)(2,1)}, u32[]{:S(2)}) copy-start(bf16[128,4096]{1,0:T(8,128)(2,1)} %all-gather.2.cloned.1.call-done) | copy-start | bytes 3145732
  124.4 78.8 %reduce-scatter.8.cloned.1.call-start = ((), (), s32[]{:S(2)}) async-start(), calls=%async_computation.8 | async-start | bytes 557056 | tf_op jit(solution)/shard_map/reduce_scatter | solution.py:85
Sparse Core Ops, SparseCore 0:
  54.8 9.8 reduce-scatter.3
  71.1 36.6 all-gather.1
  124.5 18.4 reduce-scatter.5
  147.0 56.1 reduce-scatter.7
